TPU v7x, 32 devices: a whole 2x2x4 slice. The times are simulated.
32 devices in a mesh: section: 4 (over x, core), expert: 8 (over z, y).
Axes of the slice: x: 2, y: 2, z: 4, core: 2. Of those that a mesh axis runs over, the one named last changes fastest.
Arguments:
- sent_acts: bfloat16 [4, 512, 2048], P('section', 'expert'), may hold values from -6 to 6
- stash: bfloat16 [4, 512, 2048], P('section', 'expert'), may hold values from -6 to 6
- cotangents: bfloat16 [4, 512, 2048], P('section', 'expert'), may hold values from -6 to 6
- norm_gain: bfloat16 [4, 2048], P('section'), may hold values from 0.5 to 1.5
- w_gate: bfloat16 [4, 16, 2048, 768], P('section', 'expert'), may hold values from -0.125 to 0.125
- w_up: bfloat16 [4, 16, 2048, 768], P('section', 'expert'), may hold values from -0.125 to 0.125
- w_down: bfloat16 [4, 16, 768, 2048], P('section', 'expert'), may hold values from -0.21875 to 0.21875
- routes_next: int32 [4, 512, 8], P('section', 'expert'), may hold values from 0 to 15, all different within a row; in each aligned block of 64 rows (0 to 63, 64 to 127, ..., all dimensions but the last counted through in order) at most 48 rows name the same one
- gates_next: bfloat16 [4, 512, 8], P('section', 'expert'), may hold values from 0.049804688 to 0.5
- routes_prev: int32 [4, 512, 8], P('section', 'expert'), may hold values from 0 to 15, all different within a row; in each aligned block of 64 rows (0 to 63, 64 to 127, ..., all dimensions but the last counted through in order) at most 48 rows name the same one
- gates_prev: bfloat16 [4, 512, 8], P('section', 'expert'), may hold values from 0.049804688 to 0.5
Outputs:
- fwd_out: bfloat16 [4, 512, 2048], P('section', 'expert')
- bwd_out: bfloat16 [4, 512, 2048], P('section', 'expert')
- gate_grad: bfloat16 [4, 512, 8], P('section', 'expert')
- grad_w_gate: bfloat16 [4, 16, 2048, 768], P('section', 'expert')
- grad_w_up: bfloat16 [4, 16, 2048, 768], P('section', 'expert')
- grad_w_down: bfloat16 [4, 16, 768, 2048], P('section', 'expert')
Inputs may be any that keep to these rules, and one draw needn't show every extreme that they name: `routes_next`: each row names 8 different experts. At most 48 of the 64 tokens of one device choose one expert, and in some device's tokens some expert is chosen by exactly 48. `routes_prev`: each row names 8 different experts. At most 48 of the 64 tokens of one device choose one expert, and in some device's tokens some expert is chosen by exactly 48.
All inputs are finite; a program needn't handle non-finite values.
Results may differ from a plain program's by a relative error of at most 0.008.
Values may be sent and summed in bfloat16 or wider, within the bound.
A program may use at most 128 MiB of HBM per device.

v0:
```python
import jax
import jax.numpy as jnp
from jax import lax
from jax.sharding import PartitionSpec as P

CAP = 48
EPS = 1e-06


def shifted(array, axis, by):
    count = lax.axis_size(axis)
    return lax.ppermute(array, axis, [(i, (i + by) % count) for i in range(count)])


def apply_rms_norm(rows, norm_scale_weight):
    value_entries = rows.astype(jnp.float32)
    inverse_root_scale = lax.rsqrt(
        jnp.mean(value_entries * value_entries, axis=-1, keepdims=True) + EPS
    )
    unit_rows = value_entries * inverse_root_scale
    normalized_rows = (unit_rows * norm_scale_weight.astype(jnp.float32)).astype(jnp.bfloat16)
    return (normalized_rows, unit_rows, inverse_root_scale)


def routing_tables(routes, experts_all):
    tokens_here, top = routes.shape
    flat = routes.reshape(-1)
    onehot = (flat[:, None] == jnp.arange(experts_all, dtype=jnp.int32)[None, :]).astype(jnp.int32)
    before = jnp.cumsum(onehot, axis=0) - onehot
    slot = jnp.sum(before * onehot, axis=1)
    target = flat * CAP + slot
    pick = (target[:, None] == jnp.arange(experts_all * CAP, dtype=jnp.int32)[None, :]).astype(
        jnp.float32
    )
    spread = jnp.sum(pick.reshape(tokens_here, top, -1), axis=1)
    return (pick, spread)


def pack_rows(spread, rows, experts_all, owners):
    packed = jnp.einsum(
        "tr,td->rd", spread.astype(jnp.bfloat16), rows, preferred_element_type=jnp.float32
    ).astype(jnp.bfloat16)
    return packed.reshape(owners, experts_all // owners, CAP, rows.shape[1])


def slot_values(pick, values):
    return jnp.dot(values.reshape(-1).astype(jnp.float32), pick, precision=lax.Precision.HIGHEST)


def choice_values(pick, values, top):
    return jnp.dot(pick, values.reshape(-1), precision=lax.Precision.HIGHEST).reshape(-1, top)


def expert_inputs(rows, weight_gate, weight_up):
    pre_gate = jnp.einsum("sjcd,jdf->sjcf", rows, weight_gate, preferred_element_type=jnp.float32)
    pre_up = jnp.einsum("sjcd,jdf->sjcf", rows, weight_up, preferred_element_type=jnp.float32)
    return (pre_gate, pre_up)


def expert_outputs(hidden, weight_down):
    return jnp.einsum(
        "sjcf,jfd->sjcd", hidden, weight_down, preferred_element_type=jnp.float32
    ).astype(jnp.bfloat16)


def per_device(
    sent_acts,
    stash,
    cotangents,
    norm_gain,
    w_gate,
    w_up,
    w_down,
    routes_next,
    gates_next,
    routes_prev,
    gates_prev,
):
    owners = lax.axis_size("expert")
    norm_scale_weight = norm_gain[0]
    weight_gate = w_gate[0]
    weight_up = w_up[0]
    weight_down = w_down[0]
    top = routes_next.shape[2]
    width = norm_scale_weight.shape[0]
    experts_all = weight_gate.shape[0] * owners
    tokens_here = routes_next.shape[1]
    arrived = shifted(sent_acts, "section", 1)[0]
    normalized_rows, _, _ = apply_rms_norm(arrived, norm_scale_weight)
    pick, spread = routing_tables(routes_next[0], experts_all)
    send = pack_rows(spread, normalized_rows, experts_all, owners)
    blend = jnp.sum(
        pick.reshape(tokens_here, top, -1) * gates_next[0].astype(jnp.float32)[..., None], axis=1
    ).astype(jnp.bfloat16)
    pre_gate, pre_up = expert_inputs(
        lax.all_to_all(send, "expert", split_axis=0, concat_axis=0, tiled=True),
        weight_gate,
        weight_up,
    )
    hidden = (jax.nn.silu(pre_gate) * pre_up).astype(jnp.bfloat16)
    returned = lax.all_to_all(
        expert_outputs(hidden, weight_down), "expert", split_axis=0, concat_axis=0, tiled=True
    )
    mixed = jnp.dot(
        blend, returned.reshape(experts_all * CAP, width), preferred_element_type=jnp.float32
    )
    fwd_out = (arrived.astype(jnp.float32) + mixed).astype(jnp.bfloat16)
    received_rows = shifted(cotangents, "section", -1)[0]
    previous_normalized_rows, unit_rows, inverse_root_scale = apply_rms_norm(
        stash[0], norm_scale_weight
    )
    pick_prev, spread_prev = routing_tables(routes_prev[0], experts_all)
    rows_send = pack_rows(spread_prev, previous_normalized_rows, experts_all, owners)
    plain_send = pack_rows(spread_prev, received_rows, experts_all, owners)
    gate_slots = (
        slot_values(pick_prev, gates_prev[0])
        .astype(jnp.bfloat16)
        .reshape(owners, experts_all // owners, CAP)
    )
    rows_recv, plain_recv, weight_recv = (
        lax.all_to_all(rows_send, "expert", split_axis=0, concat_axis=0, tiled=True),
        lax.all_to_all(plain_send, "expert", split_axis=0, concat_axis=0, tiled=True),
        lax.all_to_all(gate_slots, "expert", split_axis=0, concat_axis=0, tiled=True),
    )
    grad_recv = (
        weight_recv.astype(jnp.float32)[..., None] * plain_recv.astype(jnp.float32)
    ).astype(jnp.bfloat16)
    pre_gate, pre_up = expert_inputs(rows_recv, weight_gate, weight_up)
    sigma = jax.nn.sigmoid(pre_gate)
    active = pre_gate * sigma
    hidden = (active * pre_up).astype(jnp.bfloat16)
    expert_out = expert_outputs(hidden, weight_down)
    d_hidden = jnp.einsum(
        "sjcd,jfd->sjcf", grad_recv, weight_down, preferred_element_type=jnp.float32
    )
    d_gate = (d_hidden * pre_up * sigma * (1.0 + pre_gate * (1.0 - sigma))).astype(jnp.bfloat16)
    d_up = (d_hidden * active).astype(jnp.bfloat16)
    row_grad = (
        jnp.einsum("sjcf,jdf->sjcd", d_gate, weight_gate, preferred_element_type=jnp.float32)
        + jnp.einsum("sjcf,jdf->sjcd", d_up, weight_up, preferred_element_type=jnp.float32)
    ).astype(jnp.bfloat16)
    grad_gate = jnp.einsum(
        "sjcd,sjcf->jdf", rows_recv, d_gate, preferred_element_type=jnp.float32
    ).astype(jnp.bfloat16)
    grad_up = jnp.einsum(
        "sjcd,sjcf->jdf", rows_recv, d_up, preferred_element_type=jnp.float32
    ).astype(jnp.bfloat16)
    grad_down = jnp.einsum(
        "sjcf,sjcd->jfd", hidden, grad_recv, preferred_element_type=jnp.float32
    ).astype(jnp.bfloat16)
    products = jnp.sum(
        expert_out.astype(jnp.float32) * plain_recv.astype(jnp.float32), axis=-1
    ).astype(jnp.bfloat16)
    grad_back, products_back = (
        lax.all_to_all(row_grad, "expert", split_axis=0, concat_axis=0, tiled=True),
        lax.all_to_all(products, "expert", split_axis=0, concat_axis=0, tiled=True),
    )
    gate_grad = choice_values(pick_prev, products_back.astype(jnp.float32), top).astype(
        jnp.bfloat16
    )
    summed = jnp.dot(
        spread_prev.astype(jnp.bfloat16),
        grad_back.reshape(experts_all * CAP, width),
        preferred_element_type=jnp.float32,
    )
    normalized_gradient = summed * norm_scale_weight.astype(jnp.float32)
    backward_result = received_rows.astype(jnp.float32) + inverse_root_scale * (
        normalized_gradient
        - unit_rows * jnp.mean(normalized_gradient * unit_rows, axis=-1, keepdims=True)
    )
    return (
        fwd_out[None],
        backward_result.astype(jnp.bfloat16)[None],
        gate_grad[None],
        grad_gate[None],
        grad_up[None],
        grad_down[None],
    )


def solution(mesh):
    return jax.shard_map(
        per_device,
        mesh=mesh,
        in_specs=(
            P("section", "expert", None),
            P("section", "expert", None),
            P("section", "expert", None),
            P("section", None),
            P("section", "expert", None, None),
            P("section", "expert", None, None),
            P("section", "expert", None, None),
            P("section", "expert", None),
            P("section", "expert", None),
            P("section", "expert", None),
            P("section", "expert", None),
        ),
        out_specs=(
            P("section", "expert", None),
            P("section", "expert", None),
            P("section", "expert", None),
            P("section", "expert", None, None),
            P("section", "expert", None, None),
            P("section", "expert", None, None),
        ),
        check_vma=False,
    )
```

profile of v0, /device:TPU:0, one launch (start us, length us, event | category | flops | bytes accessed | tf_op | source)
XLA Modules:
  0.0 413.2 jit_solution(9998880206730808746)
XLA Ops:
  0.6 0.8 copy.152
  1.6 1.2 reduce-window.16
  3.0 0.8 copy.156
  4.4 0.7 reshape.169
  5.1 7.3 %all-to-all-start.2 = ((bf16[8,2,48]{2,1,0:T(2,128)(2,1)}), bf16[8,2,48]{2,1,0:T(2,128)(2,1)S(1)}, u32[]{:S(2)}, u32[]{:S(2)}) async-start(bf16[8,2,48]{2,1,0:T(2,128)(2,1)} %reshape.169), calls=%async_computation.2 | async-start | bytes 8192 | tf_op jit(solution)/shard_map/all_to_all | solution.py:123
  12.5 0.7 mul.177
  13.2 1.1 fusion.87
  14.9 3.7 convolution_convert_fusion
  18.9 5.7 %all-to-all-start.4 = ((bf16[8,2,48,2048]{3,2,1,0:T(8,128)(2,1)}), bf16[8,2,48,2048]{3,2,1,0:T(8,128)(2,1)S(1)}, u32[]{:S(2)}, u32[]{:S(2)}) async-start(bf16[8,2,48,2048]{3,2,1,0:T(8,128)(2,1)} %bitcast.29), calls=%async_computation.4 | async-start | bytes 6291456 | tf_op jit(solution)/shard_map/all_to_all | solution.py:121
  24.7 4.2 %collective-permute-done.1 = bf16[1,64,2048]{2,1,0:T(8,128)(2,1)S(1)} collective-permute-done((bf16[1,64,2048]{2,1,0:T(8,128)(2,1)}, bf16[1,64,2048]{2,1,0:T(8,128)(2,1)S(1)}, u32[]{:S(2)}, u32[]{:S(2)}) %collective-permute-start.1) | collective-permute-done | bytes 262176 | tf_op jit(solution)/shard_map/ppermute | solution.py:12
  28.9 2.7 convolution_convert_fusion.1
  31.6 63.2 %all-to-all-done.4 = bf16[8,2,48,2048]{3,2,1,0:T(8,128)(2,1)S(1)} async-done(((bf16[8,2,48,2048]{3,2,1,0:T(8,128)(2,1)}), bf16[8,2,48,2048]{3,2,1,0:T(8,128)(2,1)S(1)}, u32[]{:S(2)}, u32[]{:S(2)}) %all-to-all-start.4) | async-done | bytes 3145760 | tf_op jit(solution)/shard_map/all_to_all | solution.py:121
  94.8 4.6 %all-to-all-start.3 = ((bf16[8,2,48,2048]{3,2,1,0:T(8,128)(2,1)}), bf16[8,2,48,2048]{3,2,1,0:T(8,128)(2,1)}, u32[]{:S(2)}, u32[]{:S(2)}) async-start(bf16[8,2,48,2048]{3,2,1,0:T(8,128)(2,1)} %bitcast.25), calls=%async_computation.3 | async-start | bytes 6291456 | tf_op jit(solution)/shard_map/all_to_all | solution.py:122
  100.9 3.1 reduce-window.14
  104.0 1.6 slice_reduce_fusion.1
  105.6 0.7 reduce-window.15
  106.3 0.9 fusion.108
  107.2 0.7 reduce_sum.86
  107.9 1.4 bitcast_add_fusion.1
  109.3 0.7 bitcast_convert_fusion.4
  110.0 2.4 select_reduce_fusion
  112.6 2.7 convolution_convert_fusion.2
  115.3 54.2 %all-to-all-done.3 = bf16[8,2,48,2048]{3,2,1,0:T(8,128)(2,1)} async-done(((bf16[8,2,48,2048]{3,2,1,0:T(8,128)(2,1)}), bf16[8,2,48,2048]{3,2,1,0:T(8,128)(2,1)}, u32[]{:S(2)}, u32[]{:S(2)}) %all-to-all-start.3) | async-done | bytes 3145760 | tf_op jit(solution)/shard_map/all_to_all | solution.py:122
  169.5 4.6 %all-to-all-start = ((bf16[8,2,48,2048]{3,2,1,0:T(8,128)(2,1)}), bf16[8,2,48,2048]{3,2,1,0:T(8,128)(2,1)}, u32[]{:S(2)}, u32[]{:S(2)}) async-start(bf16[8,2,48,2048]{3,2,1,0:T(8,128)(2,1)} %bitcast.6), calls=%async_computation | async-start | bytes 6291456 | tf_op jit(solution)/shard_map/all_to_all | solution.py:96
  174.2 4.7 %fusion.7 = f32[2,8,48,768]{3,2,1,0:T(8,128)S(1)} fusion(bf16[1,2,2048,768]{3,2,1,0:T(8,128)(2,1)} %param.15, bf16[8,2,48,2048]{3,2,1,0:T(8,128)(2,1)S(1)} %all-to-all-done.4), kind=kOutput, calls=%fused_computation.12 | convolution fusion | flops 2415919104 | bytes 11796480 | tf_op jit(solution)/shard_map/sjcd,jdf->sjcf/dot_general | solution.py:55
  178.9 6.5 %fusion.19 = f32[2,8,48,768]{3,2,1,0:T(8,128)S(1)} fusion(bf16[1,2,768,2048]{3,2,1,0:T(8,128)(2,1)} %param.17, f32[8,2,48]{2,0,1:T(8,128)S(1)} %copy_convert_fusion, bf16[8,2,48,2048]{3,2,1,0:T(8,128)(2,1)} %all-to-all-done.3), kind=kOutput, calls=%fused_computation.24 | convolution fusion | flops 2420637696 | bytes 11799552 | tf_op jit(solution)/shard_map/sjcd,jfd->sjcf/dot_general | solution.py:133
  185.5 7.4 %fusion.50 = (bf16[8,2,48,768]{3,2,0,1:T(8,128)(2,1)S(1)}, bf16[8,2,48,768]{3,2,0,1:T(8,128)(2,1)S(1)}, bf16[8,2,48,768]{3,2,0,1:T(8,128)(2,1)}) fusion(f32[2,8,48,768]{3,2,1,0:T(8,128)S(1)} %fusion.7, f32[2,8,48,768]{3,2,1,0:T(8,128)S(1)} %fusion.19, bf16[1,2,2048,768]{3,2,1,0:T(8,128)(2,1)} %param.16, bf16[8,2,48,2048]{3,2,1,0:T(8,128)(2,1)S(1)} %all-to-all-done.4), kind=kOutput, calls=%fused_computation.52 | convolution fusion | flops 2424766464 | bytes 17694720 | tf_op jit(solution)/shard_map/sjcd,jdf->sjcf/dot_general | solution.py:56
  192.9 5.3 %fusion.1 = bf16[8,2,48]{2,0,1:T(8,128)(2,1)S(1)} fusion(bf16[8,2,48,2048]{3,2,1,0:T(8,128)(2,1)} %all-to-all-done.3, bf16[8,2,48,768]{3,2,0,1:T(8,128)(2,1)S(1)} %get-tuple-element.8, bf16[1,2,768,2048]{3,2,1,0:T(8,128)(2,1)S(1)} %bitcast.239), kind=kOutput, calls=%fused_computation.6 | convolution fusion | flops 2423782656 | bytes 10618368 | tf_op jit(solution)/shard_map/sjcf,jfd->sjcd/dot_general | solution.py:61
  198.8 4.5 %fusion.5 = f32[2,8,48,2048]{3,2,1,0:T(8,128)} fusion(bf16[8,2,48,768]{3,2,0,1:T(8,128)(2,1)S(1)} %get-tuple-element.9, bf16[1,2,2048,768]{3,2,1,0:T(8,128)(2,1)S(1)} %bitcast.237), kind=kOutput, calls=%fused_computation.10 | convolution fusion | flops 2415919104 | bytes 13762560 | tf_op jit(solution)/shard_map/sjcf,jdf->sjcd/dot_general | solution.py:139
  203.3 41.0 %all-to-all-done = bf16[8,2,48,2048]{3,2,1,0:T(8,128)(2,1)} async-done(((bf16[8,2,48,2048]{3,2,1,0:T(8,128)(2,1)}), bf16[8,2,48,2048]{3,2,1,0:T(8,128)(2,1)}, u32[]{:S(2)}, u32[]{:S(2)}) %all-to-all-start) | async-done | bytes 3145760 | tf_op jit(solution)/shard_map/all_to_all | solution.py:96
  244.3 3.5 all-to-all-start.6
  247.8 8.2 %fusion.34 = bf16[8,2,48,2048]{3,2,0,1:T(8,128)(2,1)S(1)} fusion(f32[2,8,48,2048]{3,2,1,0:T(8,128)} %fusion.5, bf16[8,2,48,768]{3,2,0,1:T(8,128)(2,1)S(1)} %copy-done.12, bf16[1,2,2048,768]{3,2,1,0:T(8,128)(2,1)} %param.16), kind=kOutput, calls=%fused_computation.35 | convolution fusion | flops 2419064832 | bytes 16908288 | tf_op jit(solution)/shard_map/sjcf,jdf->sjcd/dot_general | solution.py:140
  256.0 1.9 copy.161
  257.9 6.0 %all-to-all-start.5 = ((bf16[8,2,48,2048]{3,2,1,0:T(8,128)(2,1)}), bf16[8,2,48,2048]{3,2,1,0:T(8,128)(2,1)S(1)}, u32[]{:S(2)}, u32[]{:S(2)}) async-start(bf16[8,2,48,2048]{3,2,1,0:T(8,128)(2,1)} %copy.161), calls=%async_computation.5 | async-start | bytes 6291456 | tf_op jit(solution)/shard_map/all_to_all | solution.py:155
  263.8 7.7 %fusion.9 = f32[2,8,48,768]{3,2,1,0:T(8,128)} fusion(bf16[1,2,2048,768]{3,2,1,0:T(8,128)(2,1)} %param.15, bf16[8,2,48,2048]{3,2,1,0:T(8,128)(2,1)} %all-to-all-done), kind=kOutput, calls=%fused_computation.14 | convolution fusion | flops 2415919104 | bytes 11796480 | tf_op jit(solution)/shard_map/sjcd,jdf->sjcf/dot_general | solution.py:55
  271.6 13.0 %fusion.31 = bf16[8,2,48,2048]{3,2,0,1:T(8,128)(2,1)} fusion(bf16[1,2,768,2048]{3,2,1,0:T(8,128)(2,1)} %param.17, f32[2,8,48,768]{3,2,1,0:T(8,128)} %fusion.9, bf16[1,2,2048,768]{3,2,1,0:T(8,128)(2,1)} %param.16, bf16[8,2,48,2048]{3,2,1,0:T(8,128)(2,1)} %all-to-all-done), kind=kOutput, calls=%fused_computation.34 | convolution fusion | flops 4836950016 | bytes 21233664 | tf_op jit(solution)/shard_map/sjcf,jfd->sjcd/dot_general | solution.py:61
  284.6 4.0 copy.151
  288.6 45.6 %all-to-all-done.5 = bf16[8,2,48,2048]{3,2,1,0:T(8,128)(2,1)S(1)} async-done(((bf16[8,2,48,2048]{3,2,1,0:T(8,128)(2,1)}), bf16[8,2,48,2048]{3,2,1,0:T(8,128)(2,1)S(1)}, u32[]{:S(2)}, u32[]{:S(2)}) %all-to-all-start.5) | async-done | bytes 3145760 | tf_op jit(solution)/shard_map/all_to_all | solution.py:155
  334.2 4.7 %all-to-all-start.1 = ((bf16[8,2,48,2048]{3,2,1,0:T(8,128)(2,1)}), bf16[8,2,48,2048]{3,2,1,0:T(8,128)(2,1)}, u32[]{:S(2)}, u32[]{:S(2)}) async-start(bf16[8,2,48,2048]{3,2,1,0:T(8,128)(2,1)} %copy.151), calls=%async_computation.1 | async-start | bytes 6291456 | tf_op jit(solution)/shard_map/all_to_all | solution.py:101
  338.9 8.6 %fusion.4 = bf16[1,2,768,2048]{3,2,1,0:T(8,128)(2,1)} fusion(bf16[8,2,48,768]{3,2,0,1:T(8,128)(2,1)} %copy-done.16, f32[8,2,48]{2,0,1:T(8,128)S(1)} %copy_convert_fusion, bf16[8,2,48,2048]{3,2,1,0:T(8,128)(2,1)} %all-to-all-done.3), kind=kOutput, calls=%fused_computation.9 | convolution fusion | flops 2423783424 | bytes 10619904 | tf_op jit(solution)/shard_map/sjcf,sjcd->jfd/dot_general | solution.py:148
  347.6 5.4 %fusion.2 = bf16[1,2,2048,768]{3,2,1,0:T(8,128)(2,1)} fusion(bf16[8,2,48,2048]{3,2,1,0:T(8,128)(2,1)S(1)} %copy-done.2, bf16[8,2,48,768]{3,2,0,1:T(8,128)(2,1)S(1)} %copy-done.15), kind=kOutput, calls=%fused_computation.7 | convolution fusion | flops 2419064832 | bytes 10616832 | tf_op jit(solution)/shard_map/sjcd,sjcf->jdf/dot_general | solution.py:142
  353.0 5.4 %fusion.3 = bf16[1,2,2048,768]{3,2,1,0:T(8,128)(2,1)} fusion(bf16[8,2,48,2048]{3,2,1,0:T(8,128)(2,1)S(1)} %copy-done.2, bf16[8,2,48,768]{3,2,0,1:T(8,128)(2,1)S(1)} %copy-done.13), kind=kOutput, calls=%fused_computation.8 | convolution fusion | flops 2419064832 | bytes 10616832 | tf_op jit(solution)/shard_map/sjcd,sjcf->jdf/dot_general | solution.py:145
  359.1 3.2 fusion.70
  362.3 0.8 copy.168
  363.7 1.6 fusion.82
  365.3 43.6 %all-to-all-done.1 = bf16[8,2,48,2048]{3,2,1,0:T(8,128)(2,1)} async-done(((bf16[8,2,48,2048]{3,2,1,0:T(8,128)(2,1)}), bf16[8,2,48,2048]{3,2,1,0:T(8,128)(2,1)}, u32[]{:S(2)}, u32[]{:S(2)}) %all-to-all-start.1) | async-done | bytes 3145760 | tf_op jit(solution)/shard_map/all_to_all | solution.py:101
  409.0 3.3 fusion.57
  412.3 0.9 fusion.92
  (76 shorter events, 5.8 us)
Async XLA Ops:
  5.1 13.7 %all-to-all-start.2 = ((bf16[8,2,48]{2,1,0:T(2,128)(2,1)}), bf16[8,2,48]{2,1,0:T(2,128)(2,1)S(1)}, u32[]{:S(2)}, u32[]{:S(2)}) async-start(bf16[8,2,48]{2,1,0:T(2,128)(2,1)} %reshape.169), calls=%async_computation.2 | async-start | bytes 8192 | tf_op jit(solution)/shard_map/all_to_all | solution.py:123
  14.4 4.5 %copy-start.9 = (f32[64]{0:T(128)}, f32[64]{0:T(128)S(1)}, u32[]{:S(2)}) copy-start(f32[64]{0:T(128)S(1)} %add_rsqrt_fusion) | copy-start | bytes 772
  14.4 4.5 %copy-start.7 = (s32[64,8]{1,0:T(8,128)}, s32[64,8]{1,0:T(8,128)S(1)}, u32[]{:S(2)}) copy-start(s32[64,8]{1,0:T(8,128)S(1)} %bitcast_add_fusion) | copy-start | bytes 6148
  18.9 75.9 %all-to-all-start.4 = ((bf16[8,2,48,2048]{3,2,1,0:T(8,128)(2,1)}), bf16[8,2,48,2048]{3,2,1,0:T(8,128)(2,1)S(1)}, u32[]{:S(2)}, u32[]{:S(2)}) async-start(bf16[8,2,48,2048]{3,2,1,0:T(8,128)(2,1)} %bitcast.29), calls=%async_computation.4 | async-start | bytes 6291456 | tf_op jit(solution)/shard_map/all_to_all | solution.py:121
  24.6 4.3 %collective-permute-start.1 = (bf16[1,64,2048]{2,1,0:T(8,128)(2,1)}, bf16[1,64,2048]{2,1,0:T(8,128)(2,1)S(1)}, u32[]{:S(2)}, u32[]{:S(2)}) collective-permute-start(bf16[1,64,2048]{2,1,0:T(8,128)(2,1)} %param.13), channel_id=1, source_target_pairs={{0,24},{8,0},{16,8},{24,16},{1,25},{9,1},{17,9},{25,17},{2,26},{10... | collective-permute-start | bytes 786440 | tf_op jit(solution)/shard_map/ppermute | solution.py:12
  28.9 65.9 %copy-start.5 = (bf16[1,64,2048]{2,1,0:T(8,128)(2,1)}, bf16[1,64,2048]{2,1,0:T(8,128)(2,1)S(1)}, u32[]{:S(2)}) copy-start(bf16[1,64,2048]{2,1,0:T(8,128)(2,1)S(1)} %collective-permute-done.1) | copy-start | bytes 786436
  94.8 90.7 %copy-start.1 = (bf16[8,2,48,2048]{3,2,1,0:T(8,128)(2,1)}, bf16[8,2,48,2048]{3,2,1,0:T(8,128)(2,1)S(1)}, u32[]{:S(2)}) copy-start(bf16[8,2,48,2048]{3,2,1,0:T(8,128)(2,1)S(1)} %all-to-all-done.4) | copy-start | bytes 9437188
  94.8 4.7 %copy-start.11 = (s32[1,64,8]{1,2,0:T(8,128)S(1)}, s32[1,64,8]{1,2,0:T(8,128)}, u32[]{:S(2)}) copy-start(s32[1,64,8]{1,2,0:T(8,128)} %param.18) | copy-start | bytes 6148
  94.8 74.8 %all-to-all-start.3 = ((bf16[8,2,48,2048]{3,2,1,0:T(8,128)(2,1)}), bf16[8,2,48,2048]{3,2,1,0:T(8,128)(2,1)}, u32[]{:S(2)}, u32[]{:S(2)}) async-start(bf16[8,2,48,2048]{3,2,1,0:T(8,128)(2,1)} %bitcast.25), calls=%async_computation.3 | async-start | bytes 6291456 | tf_op jit(solution)/shard_map/all_to_all | solution.py:122
  99.3 13.1 %collective-permute-start = (bf16[1,64,2048]{2,1,0:T(8,128)(2,1)}, bf16[1,64,2048]{2,1,0:T(8,128)(2,1)S(1)}, u32[]{:S(2)}, u32[]{:S(2)}) collective-permute-start(bf16[1,64,2048]{2,1,0:T(8,128)(2,1)} %param.11), channel_id=1, source_target_pairs={{0,8},{8,16},{16,24},{24,0},{1,9},{9,17},{17,25},{25,1},{2,10},{10... | collective-permute-start | bytes 786440 | tf_op jit(solution)/shard_map/ppermute | solution.py:12
  112.5 57.1 %copy-start.3 = (bf16[1,64,2048]{2,1,0:T(8,128)(2,1)}, bf16[1,64,2048]{2,1,0:T(8,128)(2,1)S(1)}, u32[]{:S(2)}) copy-start(bf16[1,64,2048]{2,1,0:T(8,128)(2,1)S(1)} %collective-permute-done) | copy-start | bytes 786436
  169.5 74.7 %all-to-all-start = ((bf16[8,2,48,2048]{3,2,1,0:T(8,128)(2,1)}), bf16[8,2,48,2048]{3,2,1,0:T(8,128)(2,1)}, u32[]{:S(2)}, u32[]{:S(2)}) async-start(bf16[8,2,48,2048]{3,2,1,0:T(8,128)(2,1)} %bitcast.6), calls=%async_computation | async-start | bytes 6291456 | tf_op jit(solution)/shard_map/all_to_all | solution.py:96
  178.9 14.0 %slice-start.2 = ((s8[6291456]{0:T(1024)(128)(4,1)}), s8[4194304]{0:T(1024)(128)(4,1)S(1)}, s32[]{:S(2)}) async-start(s8[6291456]{0:T(1024)(128)(4,1)} %bitcast.238), calls=%async_computation.9 | async-start | bytes 8388608
  178.9 19.9 %slice-start = ((s8[6291456]{0:T(1024)(128)(4,1)}), s8[2097152]{0:T(1024)(128)(4,1)S(1)}, s32[]{:S(2)}) async-start(s8[6291456]{0:T(1024)(128)(4,1)} %bitcast.236), calls=%async_computation.7 | async-start | bytes 4194304
  185.4 7.4 %slice-start.3 = ((s8[6291456]{0:T(1024)(128)(4,1)}), s8[2097152]{0:T(1024)(128)(4,1)S(1)}, s32[]{:S(2)}) async-start(s8[6291456]{0:T(1024)(128)(4,1)} %bitcast.238), calls=%async_computation.10 | async-start | bytes 4194304
  185.5 13.3 %slice-start.1 = ((s8[6291456]{0:T(1024)(128)(4,1)}), s8[4194304]{0:T(1024)(128)(4,1)S(1)}, s32[]{:S(2)}) async-start(s8[6291456]{0:T(1024)(128)(4,1)} %bitcast.236), calls=%async_computation.8 | async-start | bytes 8388608
  192.8 5.3 %copy-start.16 = (bf16[8,2,48,768]{3,2,0,1:T(8,128)(2,1)}, bf16[8,2,48,768]{3,2,0,1:T(8,128)(2,1)S(1)}, u32[]{:S(2)}) copy-start(bf16[8,2,48,768]{3,2,0,1:T(8,128)(2,1)S(1)} %get-tuple-element.8) | copy-start | bytes 3538948
  192.8 5.9 %copy-start.14 = (bf16[8,2,48,768]{3,2,0,1:T(8,128)(2,1)}, bf16[8,2,48,768]{3,2,0,1:T(8,128)(2,1)S(1)}, u32[]{:S(2)}) copy-start(bf16[8,2,48,768]{3,2,0,1:T(8,128)(2,1)S(1)} %get-tuple-element.9) | copy-start | bytes 3538948
  198.8 49.0 %copy-start.12 = (bf16[8,2,48,768]{3,2,0,1:T(8,128)(2,1)S(1)}, bf16[8,2,48,768]{3,2,0,1:T(8,128)(2,1)}, u32[]{:S(2)}) copy-start(bf16[8,2,48,768]{3,2,0,1:T(8,128)(2,1)} %get-tuple-element.10) | copy-start | bytes 3538948
  244.3 13.6 %all-to-all-start.6 = ((bf16[8,2,48]{2,1,0:T(2,128)(2,1)}), bf16[8,2,48]{2,1,0:T(2,128)(2,1)S(1)}, u32[]{:S(2)}, u32[]{:S(2)}) async-start(bf16[8,2,48]{2,1,0:T(2,128)(2,1)} %copy.162), calls=%async_computation.6 | async-start | bytes 8192 | tf_op jit(solution)/shard_map/all_to_all | solution.py:156
  257.9 76.3 %all-to-all-start.5 = ((bf16[8,2,48,2048]{3,2,1,0:T(8,128)(2,1)}), bf16[8,2,48,2048]{3,2,1,0:T(8,128)(2,1)S(1)}, u32[]{:S(2)}, u32[]{:S(2)}) async-start(bf16[8,2,48,2048]{3,2,1,0:T(8,128)(2,1)} %copy.161), calls=%async_computation.5 | async-start | bytes 6291456 | tf_op jit(solution)/shard_map/all_to_all | solution.py:155
  334.2 74.8 %all-to-all-start.1 = ((bf16[8,2,48,2048]{3,2,1,0:T(8,128)(2,1)}), bf16[8,2,48,2048]{3,2,1,0:T(8,128)(2,1)}, u32[]{:S(2)}, u32[]{:S(2)}) async-start(bf16[8,2,48,2048]{3,2,1,0:T(8,128)(2,1)} %copy.151), calls=%async_computation.1 | async-start | bytes 6291456 | tf_op jit(solution)/shard_map/all_to_all | solution.py:101
  338.9 8.7 %copy-start.2 = (bf16[8,2,48,2048]{3,2,1,0:T(8,128)(2,1)S(1)}, bf16[8,2,48,2048]{3,2,1,0:T(8,128)(2,1)}, u32[]{:S(2)}) copy-start(bf16[8,2,48,2048]{3,2,1,0:T(8,128)(2,1)} %copy-done.1) | copy-start | bytes 9437188
  338.9 8.7 %copy-start.15 = (bf16[8,2,48,768]{3,2,0,1:T(8,128)(2,1)S(1)}, bf16[8,2,48,768]{3,2,0,1:T(8,128)(2,1)}, u32[]{:S(2)}) copy-start(bf16[8,2,48,768]{3,2,0,1:T(8,128)(2,1)} %copy-done.14) | copy-start | bytes 3538948
  347.6 5.4 %copy-start.13 = (bf16[8,2,48,768]{3,2,0,1:T(8,128)(2,1)S(1)}, bf16[8,2,48,768]{3,2,0,1:T(8,128)(2,1)}, u32[]{:S(2)}) copy-start(bf16[8,2,48,768]{3,2,0,1:T(8,128)(2,1)} %get-tuple-element.10) | copy-start | bytes 3538948
  353.0 6.1 %copy-start.8 = (s32[64,8]{1,0:T(8,128)S(1)}, s32[64,8]{1,0:T(8,128)}, u32[]{:S(2)}) copy-start(s32[64,8]{1,0:T(8,128)} %copy-done.7) | copy-start | bytes 6148
  353.0 10.7 %copy-start = (bf16[1,64,2048]{2,1,0:T(8,128)(2,1)S(1)}, bf16[1,64,2048]{2,1,0:T(8,128)(2,1)}, u32[]{:S(2)}) copy-start(bf16[1,64,2048]{2,1,0:T(8,128)(2,1)} %param.12) | copy-start | bytes 786436
  353.0 10.7 %copy-start.10 = (f32[64]{0:T(128)S(1)}, f32[64]{0:T(128)}, u32[]{:S(2)}) copy-start(f32[64]{0:T(128)} %copy-done.9) | copy-start | bytes 772
  365.3 47.0 %copy-start.4 = (f32[64,2048]{1,0:T(8,128)S(1)}, f32[64,2048]{1,0:T(8,128)}, u32[]{:S(2)}) copy-start(f32[64,2048]{1,0:T(8,128)} %get-tuple-element.12) | copy-start | bytes 1572868
  365.3 47.0 %copy-start.6 = (bf16[1,64,2048]{2,1,0:T(8,128)(2,1)S(1)}, bf16[1,64,2048]{2,1,0:T(8,128)(2,1)}, u32[]{:S(2)}) copy-start(bf16[1,64,2048]{2,1,0:T(8,128)(2,1)} %copy-done.5) | copy-start | bytes 786436
where the time goes:
time: 415 us; the launch traced here: 413 us
  waiting for transfers between devices  252 us (61%)
  matrix products  94.3 us (23%)
  starting transfers between devices  36.6 us (9%)
  local copies, waits for them, and re-layouts  14.7 us (4%)
  other arithmetic  14.6 us (4%)
    all_to_all x1, waiting for transfers between devices, per_device(): lax.all_to_all(rows_send, 'expert', split_axis=0, concat_axis=0, tiled=True)  63.2 us
    all_to_all x1, waiting for transfers between devices, per_device(): lax.all_to_all(plain_send, 'expert', split_axis=0, concat_axis=0, tiled=T...  54.2 us
    all_to_all x1, waiting for transfers between devices, per_device(): lax.all_to_all(row_grad, 'expert', split_axis=0, concat_axis=0, tiled=True)  45.6 us
    all_to_all x1, waiting for transfers between devices, per_device(): lax.all_to_all(expert_outputs(hidden, weight_down), 'expert', split_axis=...  43.6 us
    all_to_all x1, waiting for transfers between devices, per_device(): lax.all_to_all(send, 'expert', split_axis=0, concat_axis=0, tiled=True)  41 us
    dot_general x2, matrix products, expert_outputs(): jnp.einsum('sjcf,jfd->sjcd', hidden, weight_down, preferred_element_type=...  18.3 us
    dot_general x2, matrix products, expert_inputs(): jnp.einsum('sjcd,jdf->sjcf', rows, weight_gate, preferred_element_type=jn...  12.4 us
    dot_general x3, matrix products, pack_rows(): jnp.einsum('tr,td->rd', spread.astype(jnp.bfloat16), rows, preferred_elem...  9.02 us
  transfers between devices with their start and end apart: 9, of which 7 were waited for; matrix products, arithmetic and copies ran while one was open for 28% of the time, Pallas kernels for 0%

commit v1 on v0

--- a/solution.py
+++ b/solution.py
@@ -2,6 +2,7 @@
 import jax.numpy as jnp
 from jax import lax
 from jax.sharding import PartitionSpec as P
+from jax.lax import axis_index, axis_size, ppermute
 
 CAP = 48
 EPS = 1e-06
@@ -92,11 +93,26 @@
     blend = jnp.sum(
         pick.reshape(tokens_here, top, -1) * gates_next[0].astype(jnp.float32)[..., None], axis=1
     ).astype(jnp.bfloat16)
-    pre_gate, pre_up = expert_inputs(
-        lax.all_to_all(send, "expert", split_axis=0, concat_axis=0, tiled=True),
-        weight_gate,
-        weight_up,
-    )
+
+    def treat_bands(u):
+        known = axis_size("expert")
+        carry_in, k_now = (known, axis_index("expert"))
+        t1 = u.shape[0] // carry_in
+        current_arr = list(u.shape)
+        current_arr[0] = t1
+        opened = current_arr[0]
+        current_arr[0] = opened * carry_in
+        v1 = jnp.zeros(current_arr, u.dtype)
+        b = 0
+        while b < carry_in:
+            z_new = lax.dynamic_slice_in_dim(u, (k_now ^ b) * t1, t1, axis=0)
+            if b:
+                z_new = ppermute(z_new, "expert", [(dev, dev ^ b) for dev in range(carry_in)])
+            v1 = lax.dynamic_update_slice_in_dim(v1, z_new, (k_now ^ b) * opened, axis=0)
+            b = b + 1
+        return v1
+
+    pre_gate, pre_up = expert_inputs(treat_bands(send), weight_gate, weight_up)
     hidden = (jax.nn.silu(pre_gate) * pre_up).astype(jnp.bfloat16)
     returned = lax.all_to_all(
         expert_outputs(hidden, weight_down), "expert", split_axis=0, concat_axis=0, tiled=True

time: 415 us -> 440 us (1.060)
  starting transfers between devices: 36.6 us -> 70.7 us
  matrix products: 94.3 us -> 87 us
    ppermute x0 -> x7, waiting for transfers between devices: none -> 88.5 us  [treat_bands(): ppermute(z_new, 'expert', [(dev, dev ^ b) for dev in range(carry_in)])]
    all_to_all x1, waiting for transfers between devices: 54.2 us -> 0.01 us  [per_device(): lax.all_to_all(plain_send, 'expert', split_axis=0, concat_axis=0, tiled=T...]
    all_to_all x1 -> x0, waiting for transfers between devices: 41 us -> none  [per_device(): lax.all_to_all(send, 'expert', split_axis=0, concat_axis=0, tiled=True)]
    ppermute x0 -> x7, starting transfers between devices: none -> 23.4 us  [treat_bands(): ppermute(z_new, 'expert', [(dev, dev ^ b) for dev in range(carry_in)])]
    all_to_all x1, starting transfers between devices: 3.54 us -> 18.4 us  [per_device(): lax.all_to_all(products, 'expert', split_axis=0, concat_axis=0, tiled=True)]
    all_to_all x1, waiting for transfers between devices: 43.6 us -> 55.9 us  [per_device(): lax.all_to_all(expert_outputs(hidden, weight_down), 'expert', split_axis=...]
    all_to_all x1 -> x0, starting transfers between devices: 4.62 us -> none  [per_device(): lax.all_to_all(send, 'expert', split_axis=0, concat_axis=0, tiled=True)]
  transfers between devices with their start and end apart: 9 -> 15, of which waited for: 7 -> 10; matrix products, arithmetic and copies ran while one was open for 28% -> 20% of each run, Pallas kernels for 0% -> 0%
where the time goes in v1:
time: 440 us; the launch traced here: 439 us
  waiting for transfers between devices  249 us (57%)
  matrix products  87 us (20%)
  starting transfers between devices  70.7 us (16%)
  other arithmetic  15.5 us (4%)
  local copies, waits for them, and re-layouts  15.4 us (4%)
    ppermute x7, waiting for transfers between devices, treat_bands(): ppermute(z_new, 'expert', [(dev, dev ^ b) for dev in range(carry_in)])  88.5 us
    all_to_all x1, waiting for transfers between devices, per_device(): lax.all_to_all(rows_send, 'expert', split_axis=0, concat_axis=0, tiled=True)  60.3 us
    all_to_all x1, waiting for transfers between devices, per_device(): lax.all_to_all(expert_outputs(hidden, weight_down), 'expert', split_axis=...  55.9 us
    all_to_all x1, waiting for transfers between devices, per_device(): lax.all_to_all(row_grad, 'expert', split_axis=0, concat_axis=0, tiled=True)  42.9 us
    ppermute x7, starting transfers between devices, treat_bands(): ppermute(z_new, 'expert', [(dev, dev ^ b) for dev in range(carry_in)])  23.4 us
    all_to_all x1, starting transfers between devices, per_device(): lax.all_to_all(products, 'expert', split_axis=0, concat_axis=0, tiled=True)  18.4 us
    dot_general x2, matrix products, expert_outputs(): jnp.einsum('sjcf,jfd->sjcd', hidden, weight_down, preferred_element_type=...  16.1 us
  transfers between devices with their start and end apart: 15, of which 10 were waited for; matrix products, arithmetic and copies ran while one was open for 20% of the time, Pallas kernels for 0%

profile of v1, /device:TPU:0, one launch (start us, length us, event | category | flops | bytes accessed | tf_op | source)
XLA Modules:
  0.0 438.5 jit_solution(16353623859850918830)
XLA Ops:
  1.6 1.2 reduce-window.16
  5.1 7.3 %all-to-all-start.1 = ((bf16[8,2,48]{2,1,0:T(2,128)(2,1)}), bf16[8,2,48]{2,1,0:T(2,128)(2,1)S(1)}, u32[]{:S(2)}, u32[]{:S(2)}) async-start(bf16[8,2,48]{2,1,0:T(2,128)(2,1)} %reshape.169), calls=%async_computation.1 | async-start | bytes 8192 | tf_op jit(solution)/shard_map/all_to_all | solution.py:139
  13.8 1.1 fusion.81
  14.9 3.7 convolution_convert_fusion
  18.9 5.8 %all-to-all-start.3 = ((bf16[8,2,48,2048]{3,2,1,0:T(8,128)(2,1)}), bf16[8,2,48,2048]{3,2,1,0:T(8,128)(2,1)S(1)}, u32[]{:S(2)}, u32[]{:S(2)}) async-start(bf16[8,2,48,2048]{3,2,1,0:T(8,128)(2,1)} %bitcast.29), calls=%async_computation.3 | async-start | bytes 6291456 | tf_op jit(solution)/shard_map/all_to_all | solution.py:137
  26.6 3.1 reduce-window.14
  29.7 1.1 collective-permute-done.8
  30.8 3.6 convolution_convert_fusion.1
  34.4 60.3 %all-to-all-done.3 = bf16[8,2,48,2048]{3,2,1,0:T(8,128)(2,1)S(1)} async-done(((bf16[8,2,48,2048]{3,2,1,0:T(8,128)(2,1)}), bf16[8,2,48,2048]{3,2,1,0:T(8,128)(2,1)S(1)}, u32[]{:S(2)}, u32[]{:S(2)}) %all-to-all-start.3) | async-done | bytes 3145760 | tf_op jit(solution)/shard_map/all_to_all | solution.py:137
  94.8 4.6 %all-to-all-start.2 = ((bf16[8,2,48,2048]{3,2,1,0:T(8,128)(2,1)}), bf16[8,2,48,2048]{3,2,1,0:T(8,128)(2,1)}, u32[]{:S(2)}, u32[]{:S(2)}) async-start(bf16[8,2,48,2048]{3,2,1,0:T(8,128)(2,1)} %bitcast.25), calls=%async_computation.2 | async-start | bytes 6291456 | tf_op jit(solution)/shard_map/all_to_all | solution.py:138
  99.4 1.6 slice_reduce_fusion.1
  103.2 1.4 bitcast_add_fusion.1
  105.4 2.4 select_reduce_fusion
  108.0 1.1 convolution_convert_fusion.2
  109.3 1.8 collective-permute-start.1
  111.1 1.5 collective-permute-start.2
  112.9 2.6 collective-permute-start.4
  115.5 1.4 collective-permute-start.5
  117.4 16.5 %collective-permute-done.1 = bf16[1,2,48,2048]{3,2,0,1:T(8,128)(2,1)S(1)} collective-permute-done((bf16[1,2,48,2048]{3,2,0,1:T(8,128)(2,1)S(1)}, bf16[1,2,48,2048]{3,2,0,1:T(8,128)(2,1)S(1)}, u32[]{:S(2)}, u32[]{:S(2)}) %collective-permute-start.1) | collective-permute-done | bytes 393248 | tf_op jit(solution)/shard_map/ppermute | solution.py:110
  133.9 12.0 %collective-permute-start.6 = (bf16[1,2,48,2048]{3,2,0,1:T(8,128)(2,1)S(1)}, bf16[1,2,48,2048]{3,2,0,1:T(8,128)(2,1)S(1)}, u32[]{:S(2)}, u32[]{:S(2)}) collective-permute-start(bf16[1,2,48,2048]{3,2,0,1:T(8,128)(2,1)S(1)} %get-tuple-element.12), channel_id=1, source_target_pairs={{0,6},{1,7},{2,4},{3,5},{4,2},{5,3},{6,0},{7,1},{8,14},{9,15},{10,... | collective-permute-start | bytes 1179656 | tf_op jit(solution)/shard_map/ppermute | solution.py:110
  145.9 14.5 %collective-permute-done.2 = bf16[1,2,48,2048]{3,2,0,1:T(8,128)(2,1)S(1)} collective-permute-done((bf16[1,2,48,2048]{3,2,0,1:T(8,128)(2,1)S(1)}, bf16[1,2,48,2048]{3,2,0,1:T(8,128)(2,1)S(1)}, u32[]{:S(2)}, u32[]{:S(2)}) %collective-permute-start.2) | collective-permute-done | bytes 393248 | tf_op jit(solution)/shard_map/ppermute | solution.py:110
  160.4 3.8 collective-permute-start.7
  164.2 4.6 %collective-permute-done.3 = bf16[1,2,48,2048]{3,2,0,1:T(8,128)(2,1)S(1)} collective-permute-done((bf16[1,2,48,2048]{3,2,0,1:T(8,128)(2,1)S(1)}, bf16[1,2,48,2048]{3,2,0,1:T(8,128)(2,1)S(1)}, u32[]{:S(2)}, u32[]{:S(2)}) %collective-permute-start.3) | collective-permute-done | bytes 393248 | tf_op jit(solution)/shard_map/ppermute | solution.py:110
  168.9 44.5 %collective-permute-done.4 = bf16[1,2,48,2048]{3,2,0,1:T(8,128)(2,1)S(1)} collective-permute-done((bf16[1,2,48,2048]{3,2,0,1:T(8,128)(2,1)S(1)}, bf16[1,2,48,2048]{3,2,0,1:T(8,128)(2,1)S(1)}, u32[]{:S(2)}, u32[]{:S(2)}) %collective-permute-start.4) | collective-permute-done | bytes 393248 | tf_op jit(solution)/shard_map/ppermute | solution.py:110
  213.5 8.4 %collective-permute-done.5 = bf16[1,2,48,2048]{3,2,0,1:T(8,128)(2,1)S(1)} collective-permute-done((bf16[1,2,48,2048]{3,2,0,1:T(8,128)(2,1)S(1)}, bf16[1,2,48,2048]{3,2,0,1:T(8,128)(2,1)S(1)}, u32[]{:S(2)}, u32[]{:S(2)}) %collective-permute-start.5) | collective-permute-done | bytes 393248 | tf_op jit(solution)/shard_map/ppermute | solution.py:110
  222.0 1.7 copy-done.3
  223.6 4.0 fusion.9
  227.7 4.0 fusion.7
  231.7 6.5 %fusion.19 = f32[2,8,48,768]{3,2,1,0:T(8,128)S(1)} fusion(bf16[1,2,768,2048]{3,2,1,0:T(8,128)(2,1)} %param.17, f32[8,2,48]{2,0,1:T(8,128)S(1)} %copy_convert_fusion, bf16[8,2,48,2048]{3,2,1,0:T(8,128)(2,1)} %all-to-all-done.2), kind=kOutput, calls=%fused_computation.24 | convolution fusion | flops 2420637696 | bytes 11799552 | tf_op jit(solution)/shard_map/sjcd,jfd->sjcf/dot_general | solution.py:149
  238.2 7.4 %fusion.48 = (bf16[8,2,48,768]{3,2,0,1:T(8,128)(2,1)S(1)}, bf16[8,2,48,768]{3,2,0,1:T(8,128)(2,1)}, bf16[8,2,48,768]{3,2,0,1:T(8,128)(2,1)}) fusion(f32[2,8,48,768]{3,2,1,0:T(8,128)S(1)} %copy-done.13, f32[2,8,48,768]{3,2,1,0:T(8,128)S(1)} %fusion.19, bf16[1,2,2048,768]{3,2,1,0:T(8,128)(2,1)} %param.16, bf16[8,2,48,2048]{3,2,1,0:T(8,128)(2,1)S(1)} %all-to-all-done.3), kind=kOutput, calls=%fused_computation.50 | convolution fusion | flops 2424766464 | bytes 17694720 | tf_op jit(solution)/shard_map/sjcd,jdf->sjcf/dot_general | solution.py:57
  245.7 4.8 %fusion.1 = bf16[8,2,48]{2,0,1:T(8,128)(2,1)S(1)} fusion(bf16[8,2,48,2048]{3,2,1,0:T(8,128)(2,1)} %all-to-all-done.2, bf16[8,2,48,768]{3,2,0,1:T(8,128)(2,1)S(1)} %get-tuple-element.8, bf16[1,2,768,2048]{3,2,1,0:T(8,128)(2,1)S(1)} %bitcast.257), kind=kOutput, calls=%fused_computation.6 | convolution fusion | flops 2423782656 | bytes 10618368 | tf_op jit(solution)/shard_map/sjcf,jfd->sjcd/dot_general | solution.py:62
  251.1 18.4 %all-to-all-start.5 = ((bf16[8,2,48]{2,1,0:T(2,128)(2,1)}), bf16[8,2,48]{2,1,0:T(2,128)(2,1)S(1)}, u32[]{:S(2)}, u32[]{:S(2)}) async-start(bf16[8,2,48]{2,1,0:T(2,128)(2,1)} %copy.212), calls=%async_computation.5 | async-start | bytes 8192 | tf_op jit(solution)/shard_map/all_to_all | solution.py:172
  269.5 11.3 %fusion.31 = bf16[8,2,48,2048]{3,2,0,1:T(8,128)(2,1)S(1)} fusion(bf16[1,2,768,2048]{3,2,1,0:T(8,128)(2,1)} %param.17, f32[2,8,48,768]{3,2,1,0:T(8,128)} %fusion.9, bf16[8,2,48,2048]{3,2,0,1:T(8,128)(2,1)} %copy-done.3, bf16[1,2,2048,768]{3,2,1,0:T(8,128)(2,1)} %param.16), kind=kOutput, calls=%fused_computation.34 | convolution fusion | flops 4836950016 | bytes 21233664 | tf_op jit(solution)/shard_map/sjcf,jfd->sjcd/dot_general | solution.py:62
  280.8 2.1 copy.201
  282.9 6.0 %all-to-all-start = ((bf16[8,2,48,2048]{3,2,1,0:T(8,128)(2,1)}), bf16[8,2,48,2048]{3,2,1,0:T(8,128)(2,1)S(1)}, u32[]{:S(2)}, u32[]{:S(2)}) async-start(bf16[8,2,48,2048]{3,2,1,0:T(8,128)(2,1)} %copy.201), calls=%async_computation | async-start | bytes 6291456 | tf_op jit(solution)/shard_map/all_to_all | solution.py:117
  288.9 5.2 %fusion.5 = f32[2,8,48,2048]{3,2,1,0:T(8,128)S(1)} fusion(bf16[8,2,48,768]{3,2,0,1:T(8,128)(2,1)} %get-tuple-element.9, bf16[1,2,2048,768]{3,2,1,0:T(8,128)(2,1)} %param.15), kind=kOutput, calls=%fused_computation.10 | convolution fusion | flops 2415919104 | bytes 13762560 | tf_op jit(solution)/shard_map/sjcf,jdf->sjcd/dot_general | solution.py:155
  294.1 7.3 %fusion.34 = bf16[8,2,48,2048]{3,2,0,1:T(8,128)(2,1)S(1)} fusion(f32[2,8,48,2048]{3,2,1,0:T(8,128)S(1)} %fusion.5, bf16[8,2,48,768]{3,2,0,1:T(8,128)(2,1)S(1)} %copy-done.10, bf16[1,2,2048,768]{3,2,1,0:T(8,128)(2,1)} %param.16), kind=kOutput, calls=%fused_computation.35 | convolution fusion | flops 2419064832 | bytes 16908288 | tf_op jit(solution)/shard_map/sjcf,jdf->sjcd/dot_general | solution.py:156
  301.4 1.9 copy.211
  303.3 55.9 %all-to-all-done = bf16[8,2,48,2048]{3,2,1,0:T(8,128)(2,1)S(1)} async-done(((bf16[8,2,48,2048]{3,2,1,0:T(8,128)(2,1)}), bf16[8,2,48,2048]{3,2,1,0:T(8,128)(2,1)S(1)}, u32[]{:S(2)}, u32[]{:S(2)}) %all-to-all-start) | async-done | bytes 3145760 | tf_op jit(solution)/shard_map/all_to_all | solution.py:117
  359.2 4.7 %all-to-all-start.4 = ((bf16[8,2,48,2048]{3,2,1,0:T(8,128)(2,1)}), bf16[8,2,48,2048]{3,2,1,0:T(8,128)(2,1)}, u32[]{:S(2)}, u32[]{:S(2)}) async-start(bf16[8,2,48,2048]{3,2,1,0:T(8,128)(2,1)} %copy.211), calls=%async_computation.4 | async-start | bytes 6291456 | tf_op jit(solution)/shard_map/all_to_all | solution.py:171
  364.0 8.6 %fusion.4 = bf16[1,2,768,2048]{3,2,1,0:T(8,128)(2,1)} fusion(bf16[8,2,48,768]{3,2,0,1:T(8,128)(2,1)} %copy-done.14, f32[8,2,48]{2,0,1:T(8,128)S(1)} %copy_convert_fusion, bf16[8,2,48,2048]{3,2,1,0:T(8,128)(2,1)} %all-to-all-done.2), kind=kOutput, calls=%fused_computation.9 | convolution fusion | flops 2423783424 | bytes 10619904 | tf_op jit(solution)/shard_map/sjcf,sjcd->jfd/dot_general | solution.py:164
  372.6 5.4 %fusion.2 = bf16[1,2,2048,768]{3,2,1,0:T(8,128)(2,1)} fusion(bf16[8,2,48,2048]{3,2,1,0:T(8,128)(2,1)S(1)} %copy-done.2, bf16[8,2,48,768]{3,2,0,1:T(8,128)(2,1)S(1)} %copy-done.12), kind=kOutput, calls=%fused_computation.7 | convolution fusion | flops 2419064832 | bytes 10616832 | tf_op jit(solution)/shard_map/sjcd,sjcf->jdf/dot_general | solution.py:158
  378.0 5.4 %fusion.3 = bf16[1,2,2048,768]{3,2,1,0:T(8,128)(2,1)} fusion(bf16[8,2,48,2048]{3,2,1,0:T(8,128)(2,1)S(1)} %copy-done.2, bf16[8,2,48,768]{3,2,0,1:T(8,128)(2,1)S(1)} %copy-done.11), kind=kOutput, calls=%fused_computation.8 | convolution fusion | flops 2419064832 | bytes 10616832 | tf_op jit(solution)/shard_map/sjcd,sjcf->jdf/dot_general | solution.py:161
  384.1 3.2 fusion.64
  388.7 2.4 fusion.55
  391.1 42.9 %all-to-all-done.4 = bf16[8,2,48,2048]{3,2,1,0:T(8,128)(2,1)} async-done(((bf16[8,2,48,2048]{3,2,1,0:T(8,128)(2,1)}), bf16[8,2,48,2048]{3,2,1,0:T(8,128)(2,1)}, u32[]{:S(2)}, u32[]{:S(2)}) %all-to-all-start.4) | async-done | bytes 3145760 | tf_op jit(solution)/shard_map/all_to_all | solution.py:171
  434.0 2.7 fusion.76
  436.7 1.9 fusion.86
  (94 shorter events, 14.1 us)
Async XLA Ops:
  5.1 13.7 %all-to-all-start.1 = ((bf16[8,2,48]{2,1,0:T(2,128)(2,1)}), bf16[8,2,48]{2,1,0:T(2,128)(2,1)S(1)}, u32[]{:S(2)}, u32[]{:S(2)}) async-start(bf16[8,2,48]{2,1,0:T(2,128)(2,1)} %reshape.169), calls=%async_computation.1 | async-start | bytes 8192 | tf_op jit(solution)/shard_map/all_to_all | solution.py:139
  12.5 6.3 %copy-start.5 = (s32[64,8]{1,0:T(8,128)}, s32[64,8]{1,0:T(8,128)S(1)}, u32[]{:S(2)}) copy-start(s32[64,8]{1,0:T(8,128)S(1)} %bitcast_add_fusion) | copy-start | bytes 6148
  14.9 3.9 copy-start.7
  18.9 6.3 %copy-start.9 = (s32[1,64,8]{1,2,0:T(8,128)S(1)}, s32[1,64,8]{1,2,0:T(8,128)}, u32[]{:S(2)}) copy-start(s32[1,64,8]{1,2,0:T(8,128)} %param.18) | copy-start | bytes 6148
  18.9 75.9 %all-to-all-start.3 = ((bf16[8,2,48,2048]{3,2,1,0:T(8,128)(2,1)}), bf16[8,2,48,2048]{3,2,1,0:T(8,128)(2,1)S(1)}, u32[]{:S(2)}, u32[]{:S(2)}) async-start(bf16[8,2,48,2048]{3,2,1,0:T(8,128)(2,1)} %bitcast.29), calls=%async_computation.3 | async-start | bytes 6291456 | tf_op jit(solution)/shard_map/all_to_all | solution.py:137
  24.6 6.2 %collective-permute-start.8 = (bf16[1,64,2048]{2,1,0:T(8,128)(2,1)}, bf16[1,64,2048]{2,1,0:T(8,128)(2,1)}, u32[]{:S(2)}, u32[]{:S(2)}) collective-permute-start(bf16[1,64,2048]{2,1,0:T(8,128)(2,1)} %param.13), channel_id=1, source_target_pairs={{0,24},{8,0},{16,8},{24,16},{1,25},{9,1},{17,9},{25,17},{2,26},{10... | collective-permute-start | bytes 786440 | tf_op jit(solution)/shard_map/ppermute | solution.py:13
  24.7 83.1 %collective-permute-start = (bf16[1,64,2048]{2,1,0:T(8,128)(2,1)}, bf16[1,64,2048]{2,1,0:T(8,128)(2,1)S(1)}, u32[]{:S(2)}, u32[]{:S(2)}) collective-permute-start(bf16[1,64,2048]{2,1,0:T(8,128)(2,1)} %param.11), channel_id=1, source_target_pairs={{0,8},{8,16},{16,24},{24,0},{1,9},{9,17},{17,25},{25,1},{2,10},{10... | collective-permute-start | bytes 786440 | tf_op jit(solution)/shard_map/ppermute | solution.py:13
  94.8 143.4 %copy-start.1 = (bf16[8,2,48,2048]{3,2,1,0:T(8,128)(2,1)}, bf16[8,2,48,2048]{3,2,1,0:T(8,128)(2,1)S(1)}, u32[]{:S(2)}) copy-start(bf16[8,2,48,2048]{3,2,1,0:T(8,128)(2,1)S(1)} %all-to-all-done.3) | copy-start | bytes 9437188
  94.8 136.9 %all-to-all-start.2 = ((bf16[8,2,48,2048]{3,2,1,0:T(8,128)(2,1)}), bf16[8,2,48,2048]{3,2,1,0:T(8,128)(2,1)}, u32[]{:S(2)}, u32[]{:S(2)}) async-start(bf16[8,2,48,2048]{3,2,1,0:T(8,128)(2,1)} %bitcast.25), calls=%async_computation.2 | async-start | bytes 6291456 | tf_op jit(solution)/shard_map/all_to_all | solution.py:138
  107.8 1.5 copy-start.4
  109.0 114.6 %slice-start.2 = ((s8[6291456]{0:T(1024)(128)(4,1)}), s8[4194304]{0:T(1024)(128)(4,1)S(1)}, s32[]{:S(2)}) async-start(s8[6291456]{0:T(1024)(128)(4,1)} %bitcast.258), calls=%async_computation.8 | async-start | bytes 8388608
  109.3 24.6 %collective-permute-start.1 = (bf16[1,2,48,2048]{3,2,0,1:T(8,128)(2,1)S(1)}, bf16[1,2,48,2048]{3,2,0,1:T(8,128)(2,1)S(1)}, u32[]{:S(2)}, u32[]{:S(2)}) collective-permute-start(bf16[1,2,48,2048]{3,2,0,1:T(8,128)(2,1)S(1)} %get-tuple-element.17), channel_id=1, source_target_pairs={{0,1},{1,0},{2,3},{3,2},{4,5},{5,4},{6,7},{7,6},{8,9},{9,8},{10,11... | collective-permute-start | bytes 1179656 | tf_op jit(solution)/shard_map/ppermute | solution.py:110
  111.1 49.3 %collective-permute-start.2 = (bf16[1,2,48,2048]{3,2,0,1:T(8,128)(2,1)S(1)}, bf16[1,2,48,2048]{3,2,0,1:T(8,128)(2,1)S(1)}, u32[]{:S(2)}, u32[]{:S(2)}) collective-permute-start(bf16[1,2,48,2048]{3,2,0,1:T(8,128)(2,1)S(1)} %get-tuple-element.16), channel_id=1, source_target_pairs={{0,2},{1,3},{2,0},{3,1},{4,6},{5,7},{6,4},{7,5},{8,10},{9,11},{10,... | collective-permute-start | bytes 1179656 | tf_op jit(solution)/shard_map/ppermute | solution.py:110
  112.6 56.3 %collective-permute-start.3 = (bf16[1,2,48,2048]{3,2,0,1:T(8,128)(2,1)S(1)}, bf16[1,2,48,2048]{3,2,0,1:T(8,128)(2,1)S(1)}, u32[]{:S(2)}, u32[]{:S(2)}) collective-permute-start(bf16[1,2,48,2048]{3,2,0,1:T(8,128)(2,1)S(1)} %get-tuple-element.15), channel_id=1, source_target_pairs={{0,3},{1,2},{2,1},{3,0},{4,7},{5,6},{6,5},{7,4},{8,11},{9,10},{10,... | collective-permute-start | bytes 1179656 | tf_op jit(solution)/shard_map/ppermute | solution.py:110
  112.9 100.5 %collective-permute-start.4 = (bf16[1,2,48,2048]{3,2,0,1:T(8,128)(2,1)S(1)}, bf16[1,2,48,2048]{3,2,0,1:T(8,128)(2,1)S(1)}, u32[]{:S(2)}, u32[]{:S(2)}) collective-permute-start(bf16[1,2,48,2048]{3,2,0,1:T(8,128)(2,1)S(1)} %get-tuple-element.14), channel_id=1, source_target_pairs={{0,4},{1,5},{2,6},{3,7},{4,0},{5,1},{6,2},{7,3},{8,12},{9,13},{10,... | collective-permute-start | bytes 1179656 | tf_op jit(solution)/shard_map/ppermute | solution.py:110
  115.5 108.1 %slice-start.3 = ((s8[6291456]{0:T(1024)(128)(4,1)}), s8[2097152]{0:T(1024)(128)(4,1)S(1)}, s32[]{:S(2)}) async-start(s8[6291456]{0:T(1024)(128)(4,1)} %bitcast.258), calls=%async_computation.9 | async-start | bytes 4194304
  115.5 106.3 %collective-permute-start.5 = (bf16[1,2,48,2048]{3,2,0,1:T(8,128)(2,1)S(1)}, bf16[1,2,48,2048]{3,2,0,1:T(8,128)(2,1)S(1)}, u32[]{:S(2)}, u32[]{:S(2)}) collective-permute-start(bf16[1,2,48,2048]{3,2,0,1:T(8,128)(2,1)S(1)} %get-tuple-element.13), channel_id=1, source_target_pairs={{0,5},{1,4},{2,7},{3,6},{4,1},{5,0},{6,3},{7,2},{8,13},{9,12},{10,... | collective-permute-start | bytes 1179656 | tf_op jit(solution)/shard_map/ppermute | solution.py:110
  133.9 87.9 %collective-permute-start.6 = (bf16[1,2,48,2048]{3,2,0,1:T(8,128)(2,1)S(1)}, bf16[1,2,48,2048]{3,2,0,1:T(8,128)(2,1)S(1)}, u32[]{:S(2)}, u32[]{:S(2)}) collective-permute-start(bf16[1,2,48,2048]{3,2,0,1:T(8,128)(2,1)S(1)} %get-tuple-element.12), channel_id=1, source_target_pairs={{0,6},{1,7},{2,4},{3,5},{4,2},{5,3},{6,0},{7,1},{8,14},{9,15},{10,... | collective-permute-start | bytes 1179656 | tf_op jit(solution)/shard_map/ppermute | solution.py:110
  160.4 61.5 %collective-permute-start.7 = (bf16[1,2,48,2048]{3,2,0,1:T(8,128)(2,1)S(1)}, bf16[1,2,48,2048]{3,2,0,1:T(8,128)(2,1)S(1)}, u32[]{:S(2)}, u32[]{:S(2)}) collective-permute-start(bf16[1,2,48,2048]{3,2,0,1:T(8,128)(2,1)S(1)} %get-tuple-element.11), channel_id=1, source_target_pairs={{0,7},{1,6},{2,5},{3,4},{4,3},{5,2},{6,1},{7,0},{8,15},{9,14},{10,... | collective-permute-start | bytes 1179656 | tf_op jit(solution)/shard_map/ppermute | solution.py:110
  221.9 1.7 copy-start.3
  231.7 6.5 %copy-start.13 = (f32[2,8,48,768]{3,2,1,0:T(8,128)S(1)}, f32[2,8,48,768]{3,2,1,0:T(8,128)}, u32[]{:S(2)}) copy-start(f32[2,8,48,768]{3,2,1,0:T(8,128)} %fusion.7) | copy-start | bytes 7077892
  231.7 14.0 %slice-start = ((s8[6291456]{0:T(1024)(128)(4,1)}), s8[2097152]{0:T(1024)(128)(4,1)S(1)}, s32[]{:S(2)}) async-start(s8[6291456]{0:T(1024)(128)(4,1)} %bitcast.256), calls=%async_computation.6 | async-start | bytes 4194304
  238.2 7.4 %slice-start.1 = ((s8[6291456]{0:T(1024)(128)(4,1)}), s8[4194304]{0:T(1024)(128)(4,1)S(1)}, s32[]{:S(2)}) async-start(s8[6291456]{0:T(1024)(128)(4,1)} %bitcast.256), calls=%async_computation.7 | async-start | bytes 8388608
  245.7 4.8 %copy-start.14 = (bf16[8,2,48,768]{3,2,0,1:T(8,128)(2,1)}, bf16[8,2,48,768]{3,2,0,1:T(8,128)(2,1)S(1)}, u32[]{:S(2)}) copy-start(bf16[8,2,48,768]{3,2,0,1:T(8,128)(2,1)S(1)} %get-tuple-element.8) | copy-start | bytes 3538948
  251.1 31.8 %all-to-all-start.5 = ((bf16[8,2,48]{2,1,0:T(2,128)(2,1)}), bf16[8,2,48]{2,1,0:T(2,128)(2,1)S(1)}, u32[]{:S(2)}, u32[]{:S(2)}) async-start(bf16[8,2,48]{2,1,0:T(2,128)(2,1)} %copy.212), calls=%async_computation.5 | async-start | bytes 8192 | tf_op jit(solution)/shard_map/all_to_all | solution.py:172
  282.9 76.3 %all-to-all-start = ((bf16[8,2,48,2048]{3,2,1,0:T(8,128)(2,1)}), bf16[8,2,48,2048]{3,2,1,0:T(8,128)(2,1)S(1)}, u32[]{:S(2)}, u32[]{:S(2)}) async-start(bf16[8,2,48,2048]{3,2,1,0:T(8,128)(2,1)} %copy.201), calls=%async_computation | async-start | bytes 6291456 | tf_op jit(solution)/shard_map/all_to_all | solution.py:117
  288.9 5.2 %copy-start.10 = (bf16[8,2,48,768]{3,2,0,1:T(8,128)(2,1)S(1)}, bf16[8,2,48,768]{3,2,0,1:T(8,128)(2,1)}, u32[]{:S(2)}) copy-start(bf16[8,2,48,768]{3,2,0,1:T(8,128)(2,1)} %get-tuple-element.10) | copy-start | bytes 3538948
  359.2 74.8 %all-to-all-start.4 = ((bf16[8,2,48,2048]{3,2,1,0:T(8,128)(2,1)}), bf16[8,2,48,2048]{3,2,1,0:T(8,128)(2,1)}, u32[]{:S(2)}, u32[]{:S(2)}) async-start(bf16[8,2,48,2048]{3,2,1,0:T(8,128)(2,1)} %copy.211), calls=%async_computation.4 | async-start | bytes 6291456 | tf_op jit(solution)/shard_map/all_to_all | solution.py:171
  363.9 8.7 %copy-start.2 = (bf16[8,2,48,2048]{3,2,1,0:T(8,128)(2,1)S(1)}, bf16[8,2,48,2048]{3,2,1,0:T(8,128)(2,1)}, u32[]{:S(2)}) copy-start(bf16[8,2,48,2048]{3,2,1,0:T(8,128)(2,1)} %copy-done.1) | copy-start | bytes 9437188
  363.9 8.7 %copy-start.12 = (bf16[8,2,48,768]{3,2,0,1:T(8,128)(2,1)S(1)}, bf16[8,2,48,768]{3,2,0,1:T(8,128)(2,1)}, u32[]{:S(2)}) copy-start(bf16[8,2,48,768]{3,2,0,1:T(8,128)(2,1)} %get-tuple-element.9) | copy-start | bytes 3538948
  372.6 5.4 %copy-start.11 = (bf16[8,2,48,768]{3,2,0,1:T(8,128)(2,1)S(1)}, bf16[8,2,48,768]{3,2,0,1:T(8,128)(2,1)}, u32[]{:S(2)}) copy-start(bf16[8,2,48,768]{3,2,0,1:T(8,128)(2,1)} %get-tuple-element.10) | copy-start | bytes 3538948
  378.0 6.1 %copy-start.6 = (s32[64,8]{1,0:T(8,128)S(1)}, s32[64,8]{1,0:T(8,128)}, u32[]{:S(2)}) copy-start(s32[64,8]{1,0:T(8,128)} %copy-done.5) | copy-start | bytes 6148
  383.4 50.6 %copy-start = (bf16[1,64,2048]{2,1,0:T(8,128)(2,1)S(1)}, bf16[1,64,2048]{2,1,0:T(8,128)(2,1)}, u32[]{:S(2)}) copy-start(bf16[1,64,2048]{2,1,0:T(8,128)(2,1)} %param.12) | copy-start | bytes 786436
  383.4 50.6 %copy-start.8 = (f32[64]{0:T(128)S(1)}, f32[64]{0:T(128)}, u32[]{:S(2)}) copy-start(f32[64]{0:T(128)} %copy-done.7) | copy-start | bytes 772
